TPU v7x, 32 devices: a whole 2x2x4 slice. The times are simulated.
32 devices in a mesh: row: 4 (over z), col: 8 (over y, x, core).
Axes of the slice: x: 2, y: 2, z: 4, core: 2. Of those that a mesh axis runs over, the one named last changes fastest.
Arguments:
- features: bfloat16 [8, 1024, 256], P('col', 'row'), may hold values from -6 to 6
- weight: bfloat16 [256, 256], replicated, may hold values from -0.375 to 0.375
- cotangent: bfloat16 [8192, 256], P(('row', 'col')), may hold values from -6 to 6
- blk_vals: bfloat16 [4, 8, 192, 128, 128], P('row', 'col'), may hold values from -0.0546875 to 0.0546875
- blk_rows: int32 [4, 8, 192], P('row', 'col'), may hold values from 0 to 15
- blk_cols: int32 [4, 8, 192], P('row', 'col'), may hold values from 0 to 7
- blk_count: int32 [4, 8], P('row', 'col'), may hold values from 24 to 192, as said below
Outputs:
- activated: bfloat16 [8192, 256], P(('row', 'col'))
- grad_weight: float32 [256, 256], replicated
- grad_features: bfloat16 [8, 1024, 256], P('col', 'row')
Inputs may be any that keep to these rules, and one draw needn't show every extreme that they name: Only the first blk_count slots of a panel pair are used; a pair whose row and column node ranges intersect uses all 192, every other pair at most 96.
All inputs are finite; a program needn't handle non-finite values.
Results may differ from a plain program's by a relative error of at most 0.0059.
Values may be sent and summed in bfloat16 or wider, within the bound.
A program may use at most 128 MiB of HBM per device.

v0:
```python
import jax
import jax.numpy as jnp
from jax import lax
from jax.sharding import PartitionSpec as P


def block_terms(values, index, source, live_count, transpose):
    total_slots = values.shape[0]
    group = 64
    width = source.shape[-1]
    side = values.shape[-1]
    if transpose:
        form = "bji,bjf->bif"
    else:
        form = "bij,bjf->bif"

    def one_group(group_index, buffer):
        first = group_index * group
        block_vals = lax.dynamic_slice_in_dim(values, first, group, 0)
        block_ids = lax.dynamic_slice_in_dim(index, first, group, 0)
        picked = jnp.take(source, block_ids, axis=0)
        product = jnp.einsum(form, block_vals, picked, preferred_element_type=jnp.float32)
        alive = first + jnp.arange(group, dtype=jnp.int32) < live_count
        product = jnp.where(alive[:, None, None], product, 0.0)
        return lax.dynamic_update_slice_in_dim(buffer, product, first, 0)

    buffer = jnp.zeros((total_slots, side, width), jnp.float32)
    groups = total_slots // group
    return lax.fori_loop(0, groups, one_group, buffer)


def per_device(features, weight, cotangent, blk_vals, blk_rows, blk_cols, blk_count):
    rows_here = cotangent.shape[0]
    width = cotangent.shape[1]
    side = blk_vals.shape[-1]
    row_blocks = rows_here * lax.axis_size("col") // side
    col_blocks = rows_here * lax.axis_size("row") // side
    values = blk_vals[0, 0]
    row_ids = blk_rows[0, 0]
    col_ids = blk_cols[0, 0]
    live_count = blk_count[0, 0]
    panel = lax.all_gather(features, "row", axis=1, tiled=True)
    source = panel.reshape(col_blocks, side, width)
    products = block_terms(values, col_ids, source, live_count, False)
    partial_rows = jax.ops.segment_sum(products, row_ids, num_segments=row_blocks)
    own_rows = lax.psum_scatter(
        partial_rows.reshape(row_blocks * side, width), "col", scatter_dimension=0, tiled=True
    )
    aggregated = own_rows.astype(jnp.bfloat16)
    pre = jnp.dot(aggregated, weight, preferred_element_type=jnp.float32)
    sigma = jax.nn.sigmoid(pre)
    activated = (pre * sigma).astype(jnp.bfloat16)
    grad_pre = (cotangent.astype(jnp.float32) * sigma * (1.0 + pre * (1.0 - sigma))).astype(
        jnp.bfloat16
    )
    local_weight = lax.dot_general(
        aggregated, grad_pre, (((0,), (0,)), ((), ())), preferred_element_type=jnp.float32
    )
    grad_weight = lax.psum(local_weight, ("row", "col"))
    grad_agg = lax.dot_general(
        grad_pre, weight, (((1,), (1,)), ((), ())), preferred_element_type=jnp.float32
    ).astype(jnp.bfloat16)
    grad_rows = lax.all_gather(grad_agg, "col", axis=0, tiled=True)
    grad_source = grad_rows.reshape(row_blocks, side, width)
    back_products = block_terms(values, row_ids, grad_source, live_count, True)
    partial_cols = jax.ops.segment_sum(back_products, col_ids, num_segments=col_blocks)
    own_cols = lax.psum_scatter(
        partial_cols.reshape(col_blocks * side, width), "row", scatter_dimension=0, tiled=True
    )
    grad_features = own_cols.astype(jnp.bfloat16).reshape(1, rows_here, width)
    return (activated, grad_weight, grad_features)


def solution(mesh):
    return jax.shard_map(
        per_device,
        mesh=mesh,
        in_specs=(
            P("col", "row", None),
            P(),
            P(("row", "col"), None),
            P("row", "col", None, None, None),
            P("row", "col", None),
            P("row", "col", None),
            P("row", "col"),
        ),
        out_specs=(P(("row", "col"), None), P(), P("col", "row", None)),
        check_vma=False,
    )
```

profile of v0, /device:TPU:0, one launch (start us, length us, event | category | flops | bytes accessed | tf_op | source)
XLA Modules:
  0.0 423.9 jit_solution(15833494370647342353)
XLA Ops:
  7.2 17.6 %all_gather.6 = bf16[1,1024,256]{2,1,0:T(8,128)(2,1)S(1)} all-gather(bf16[1,256,256]{2,1,0:T(8,128)(2,1)} %param.11), channel_id=1, replica_groups=mesh['row'=4,'col'=8] {'row'}, dimensions={1}, use_global_device_ids=true | all-gather | bytes 655360 | tf_op jit(solution)/shard_map/all_gather | solution.py:42
  24.8 11.5 %broadcast.44.clone = f32[192,128,256]{2,1,0:T(8,128)} broadcast(f32[]{:T(128)} %constant.131.clone.1), dimensions={} | broadcast | bytes 25165828 | tf_op jit(solution)/shard_map/broadcast.3
  36.3 32.7 %while.26 = (s32[]{:T(128)}, f32[192,128,256]{2,1,0:T(8,128)}, s32[]{:T(128)}, bf16[192,128,128]{2,1,0:T(8,128)(2,1)}, s32[192]{0:T(256)S(1)}, /*index=5*/bf16[8...) while((s32[]{:T(128)}, f32[192,128,256]{2,1,0:T(8,128)}, s32[]{:T(128)}, ...), condition=%wide.region_1.0_spmd, body=%wide.region_0.1_spmd.sunk | while | flops 541066752 | bytes 23075232 | solution.py:29
  37.1 2.8 gather_fusion
  39.8 7.4 %select_dynamic-update-slice_fusion.4 = f32[192,128,256]{2,1,0:T(8,128)} fusion(f32[192,128,256]{2,1,0:T(8,128)} %get-tuple-element.358, s32[]{:T(128)S(6)} %select_n.88, pred[64]{0:T(512)(128)(4,1)S(1)} %get-tuple-element.335, bf16[64,128,256]{2,1,0:T(8,128)(2,1)} %gather_fusion, pred[64]{0:T(512)(128)(4,1)S(1)} %get-tuple-element.337, ...), kind=kOutput, calls=%fused_computation.4.clone.1 | convolution fusion | flops 541065216 | bytes 14681216 | tf_op jit(solution)/shard_map/while/body/eval_jaxpr/bij,bjf->bif/dot_general | solution.py:22
  47.9 2.8 gather_fusion
  50.7 7.4 %select_dynamic-update-slice_fusion.4 = f32[192,128,256]{2,1,0:T(8,128)} fusion(f32[192,128,256]{2,1,0:T(8,128)} %get-tuple-element.358, s32[]{:T(128)S(6)} %select_n.88, pred[64]{0:T(512)(128)(4,1)S(1)} %get-tuple-element.335, bf16[64,128,256]{2,1,0:T(8,128)(2,1)} %gather_fusion, pred[64]{0:T(512)(128)(4,1)S(1)} %get-tuple-element.337, ...), kind=kOutput, calls=%fused_computation.4.clone.1 | convolution fusion | flops 541065216 | bytes 14681216 | tf_op jit(solution)/shard_map/while/body/eval_jaxpr/bij,bjf->bif/dot_general | solution.py:22
  58.8 2.8 gather_fusion
  61.6 7.4 %select_dynamic-update-slice_fusion.4 = f32[192,128,256]{2,1,0:T(8,128)} fusion(f32[192,128,256]{2,1,0:T(8,128)} %get-tuple-element.358, s32[]{:T(128)S(6)} %select_n.88, pred[64]{0:T(512)(128)(4,1)S(1)} %get-tuple-element.335, bf16[64,128,256]{2,1,0:T(8,128)(2,1)} %gather_fusion, pred[64]{0:T(512)(128)(4,1)S(1)} %get-tuple-element.337, ...), kind=kOutput, calls=%fused_computation.4.clone.1 | convolution fusion | flops 541065216 | bytes 14681216 | tf_op jit(solution)/shard_map/while/body/eval_jaxpr/bij,bjf->bif/dot_general | solution.py:22
  69.2 36.1 %scatter_fusion = f32[16,128,256]{2,1,0:T(8,128)S(1)} fusion(f32[16,128,256]{2,1,0:T(8,128)S(1)} %broadcast_in_dim.108, s32[192]{0:T(256)S(1)} %bitcast.22, f32[192,128,256]{2,1,0:T(8,128)} %get-tuple-element.221), kind=kCustom, calls=%fused_computation.2 | custom fusion | flops 6291456 | bytes 75498240 | tf_op jit(solution)/shard_map/scatter-add | solution.py:45
  106.7 43.0 %reduce-scatter.3.cloned.1.call-done = f32[256,256]{1,0:T(8,128)} async-done(((f32[2048,256]{1,0:T(8,128)}), f32[256,256]{1,0:T(8,128)}) %reduce-scatter.3.cloned.1.call-update) | async-done | bytes 262160 | tf_op jit(solution)/shard_map/reduce_scatter | solution.py:46
  152.5 8.6 %copy.10 = bf16[1,1,192,128,128]{3,4,2,1,0:T(8,128)(2,1)} copy(bf16[1,1,192,128,128]{4,3,2,1,0:T(8,128)(2,1)} %bitcast.20) | data formatting | bytes 12582912 | tf_op args[3]
  161.0 14.9 %all-gather.2.cloned.1.call-done = bf16[2048,256]{1,0:T(8,128)(2,1)} async-done(((bf16[256,256]{1,0:T(8,128)(2,1)}), bf16[2048,256]{1,0:T(8,128)(2,1)}) %all-gather.2.cloned.1.call-update) | async-done | bytes 1048592 | tf_op jit(solution)/shard_map/all_gather | solution.py:63
  176.0 11.5 %broadcast.44 = f32[192,128,256]{2,1,0:T(8,128)} broadcast(f32[]{:T(128)} %constant.131.clone.1), dimensions={} | broadcast | bytes 25165828 | tf_op jit(solution)/shard_map/broadcast.3
  187.4 32.7 %while.27 = (s32[]{:T(128)}, f32[192,128,256]{2,1,0:T(8,128)}, s32[]{:T(128)}, bf16[192,128,128]{1,2,0:T(8,128)(2,1)}, s32[192]{0:T(256)S(1)}, /*index=5*/bf16[1...) while((s32[]{:T(128)}, f32[192,128,256]{2,1,0:T(8,128)}, s32[]{:T(128)}, ...), condition=%wide.region_6.7_spmd, body=%wide.region_5.6_spmd.sunk | while | flops 541066752 | bytes 23075232 | solution.py:29
  188.2 2.8 gather_fusion.1
  191.0 7.4 %select_dynamic-update-slice_fusion.5 = f32[192,128,256]{2,1,0:T(8,128)} fusion(f32[192,128,256]{2,1,0:T(8,128)} %get-tuple-element.388, s32[]{:T(128)S(6)} %select_n.91, pred[64]{0:T(512)(128)(4,1)S(1)} %get-tuple-element.344, bf16[64,128,256]{2,1,0:T(8,128)(2,1)} %gather_fusion.1, pred[64]{0:T(512)(128)(4,1)S(1)} %get-tuple-element.346, ...), kind=kOutput, calls=%fused_computation.16.clone.1 | convolution fusion | flops 541065216 | bytes 14681216 | tf_op jit(solution)/shard_map/while/body/eval_jaxpr/bji,bjf->bif/dot_general | solution.py:22
  199.1 2.8 gather_fusion.1
  201.8 7.4 %select_dynamic-update-slice_fusion.5 = f32[192,128,256]{2,1,0:T(8,128)} fusion(f32[192,128,256]{2,1,0:T(8,128)} %get-tuple-element.388, s32[]{:T(128)S(6)} %select_n.91, pred[64]{0:T(512)(128)(4,1)S(1)} %get-tuple-element.344, bf16[64,128,256]{2,1,0:T(8,128)(2,1)} %gather_fusion.1, pred[64]{0:T(512)(128)(4,1)S(1)} %get-tuple-element.346, ...), kind=kOutput, calls=%fused_computation.16.clone.1 | convolution fusion | flops 541065216 | bytes 14681216 | tf_op jit(solution)/shard_map/while/body/eval_jaxpr/bji,bjf->bif/dot_general | solution.py:22
  210.0 2.8 gather_fusion.1
  212.7 7.4 %select_dynamic-update-slice_fusion.5 = f32[192,128,256]{2,1,0:T(8,128)} fusion(f32[192,128,256]{2,1,0:T(8,128)} %get-tuple-element.388, s32[]{:T(128)S(6)} %select_n.91, pred[64]{0:T(512)(128)(4,1)S(1)} %get-tuple-element.344, bf16[64,128,256]{2,1,0:T(8,128)(2,1)} %gather_fusion.1, pred[64]{0:T(512)(128)(4,1)S(1)} %get-tuple-element.346, ...), kind=kOutput, calls=%fused_computation.16.clone.1 | convolution fusion | flops 541065216 | bytes 14681216 | tf_op jit(solution)/shard_map/while/body/eval_jaxpr/bji,bjf->bif/dot_general | solution.py:22
  220.2 36.0 %scatter_fusion.1 = f32[8,128,256]{2,1,0:T(8,128)S(1)} fusion(f32[8,128,256]{2,1,0:T(8,128)S(1)} %broadcast_in_dim.109, s32[192]{0:T(256)S(1)} %get-tuple-element.427, f32[192,128,256]{2,1,0:T(8,128)} %get-tuple-element.222), kind=kCustom, calls=%fused_computation.3 | custom fusion | flops 6291456 | bytes 75498240 | tf_op jit(solution)/shard_map/scatter-add | solution.py:66
  258.2 26.4 %reduce-scatter.5.cloned.1.call-done = f32[256,256]{1,0:T(8,128)} async-done(((f32[1024,256]{1,0:T(8,128)}), f32[256,256]{1,0:T(8,128)}) %reduce-scatter.5.cloned.1.call-update) | async-done | bytes 262160 | tf_op jit(solution)/shard_map/reduce_scatter | solution.py:67
  286.3 129.4 %all-reduce.2.cloned.1.call-done = f32[256,256]{1,0:T(8,128)} async-done(((f32[256,256]{1,0:T(8,128)}), f32[256,256]{1,0:T(8,128)}) %all-reduce.2.cloned.1.call-update) | async-done | bytes 262160 | tf_op jit(solution)/shard_map/psum | solution.py:59
  (45 shorter events, 14.2 us)
Async XLA Ops:
  7.2 142.5 %copy-start = (bf16[256,256]{1,0:T(8,128)(2,1)S(1)}, bf16[256,256]{1,0:T(8,128)(2,1)}, u32[]{:S(2)}) copy-start(bf16[256,256]{1,0:T(8,128)(2,1)} %param.12) | copy-start | bytes 393220
  7.2 142.5 %reduce-scatter.3.cloned.1.call-start = ((), (), s32[]{:S(2)}) async-start(), calls=%async_computation.2 | async-start | bytes 2359296 | tf_op jit(solution)/shard_map/reduce_scatter | solution.py:46
  24.8 11.5 %copy-start.7 = (s32[1,1,192]{2,1,0:T(1,128)S(1)}, s32[1,1,192]{2,1,0:T(1,128)}, u32[]{:S(2)}) copy-start(s32[1,1,192]{2,1,0:T(1,128)} %param.16) | copy-start | bytes 2308
  36.3 32.9 %copy-start.6 = (s32[1,1,192]{2,1,0:T(1,128)S(1)}, s32[1,1,192]{2,1,0:T(1,128)}, u32[]{:S(2)}) copy-start(s32[1,1,192]{2,1,0:T(1,128)} %param.15) | copy-start | bytes 2308
  69.2 80.4 %copy-start.8 = (bf16[256,256]{1,0:T(8,128)(2,1)S(1)}, bf16[256,256]{1,0:T(8,128)(2,1)}, u32[]{:S(2)}) copy-start(bf16[256,256]{1,0:T(8,128)(2,1)} %param.13) | copy-start | bytes 393220
  105.3 1.3 copy-start.4
  106.6 69.3 %all-gather.2.cloned.1.call-start = ((), (), s32[]{:S(2)}) async-start(), calls=%async_computation.4 | async-start | bytes 1179648 | tf_op jit(solution)/shard_map/all_gather | solution.py:63
  152.4 132.2 %reduce-scatter.5.cloned.1.call-start = ((), (), s32[]{:S(2)}) async-start(), calls=%async_computation.5 | async-start | bytes 1310720 | tf_op jit(solution)/shard_map/reduce_scatter | solution.py:67
  176.0 11.5 %copy-start.3 = (bf16[2048,256]{1,0:T(8,128)(2,1)S(1)}, bf16[2048,256]{1,0:T(8,128)(2,1)}, u32[]{:S(2)}) copy-start(bf16[2048,256]{1,0:T(8,128)(2,1)} %all-gather.2.cloned.1.call-done) | copy-start | bytes 3145732
  220.2 37.1 %copy-start.5 = (f32[256,256]{1,0:T(8,128)S(1)}, f32[256,256]{1,0:T(8,128)}, u32[]{:S(2)}) copy-start(f32[256,256]{1,0:T(8,128)} %reduce-scatter.3.cloned.1.call-done) | copy-start | bytes 786436
  220.2 197.1 %copy-start.1 = (bf16[256,256]{1,0:T(8,128)(2,1)S(1)}, bf16[256,256]{1,0:T(8,128)(2,1)}, u32[]{:S(2)}) copy-start(bf16[256,256]{1,0:T(8,128)(2,1)} %param.12) | copy-start | bytes 393220
  256.2 1.0 copy-start.2
  257.2 158.5 %all-reduce.2.cloned.1.call-start = ((), (), s32[]{:S(2)}) async-start(), calls=%async_computation.3 | async-start | bytes 524288 | tf_op jit(solution)/shard_map/psum | solution.py:59
Sparse Core Ops, SparseCore 0:
  106.7 42.8 reduce-scatter.2
  152.6 23.3 all-gather.1
  257.3 27.2 reduce-scatter.4
  290.6 125.0 all-reduce.1
where the time goes:
time: 425 us; the launch traced here: 424 us
  waiting for transfers between devices  214 us (50%)
  other arithmetic  78.1 us (18%)
  local copies, waits for them, and re-layouts  52.5 us (12%)
  matrix products  47.9 us (11%)
  blocking collectives  17.6 us (4%)
  between operations  13.9 us (3%)
    psum x1, waiting for transfers between devices, per_device(): grad_weight = lax.psum(local_weight, ('row', 'col'))  129 us
    dot_general x6, matrix products, one_group(): jnp.einsum(form, block_vals, picked, preferred_element_type=jnp.float32)  44.3 us
    reduce_scatter x1, waiting for transfers between devices, per_device(): lax.psum_scatter(partial_rows.reshape(row_blocks * side, width), 'col', s...  43 us
    scatter-add x1, other arithmetic, per_device(): jax.ops.segment_sum(products, row_ids, num_segments=row_blocks)  36.1 us
    scatter-add x1, other arithmetic, per_device(): jax.ops.segment_sum(back_products, col_ids, num_segments=col_blocks)  36 us
    reduce_scatter x1, waiting for transfers between devices, per_device(): lax.psum_scatter(partial_cols.reshape(col_blocks * side, width), 'row', s...  26.4 us
    another operation x2, local copies, waits for them, and re-layouts  23 us
    all_gather x1, blocking collectives, per_device(): panel = lax.all_gather(features, 'row', axis=1, tiled=True)  17.6 us
  transfers between devices with their start and end apart: 4, of which 4 were waited for; matrix products, arithmetic and copies ran while one was open for 3% of the time, Pallas kernels for 0%

commit v1 on v0

--- a/solution.py
+++ b/solution.py
@@ -56,7 +56,7 @@
     local_weight = lax.dot_general(
         aggregated, grad_pre, (((0,), (0,)), ((), ())), preferred_element_type=jnp.float32
     )
-    grad_weight = lax.psum(local_weight, ("row", "col"))
+    grad_weight = jnp.sum(lax.all_gather(local_weight, axis_name=("row", "col")), axis=0)
     grad_agg = lax.dot_general(
         grad_pre, weight, (((1,), (1,)), ((), ())), preferred_element_type=jnp.float32
     ).astype(jnp.bfloat16)

time: 425 us -> 376 us (0.88)
  waiting for transfers between devices: 214 us -> 162 us
  other arithmetic: 78.1 us -> 82.7 us
    psum x1 -> x0, waiting for transfers between devices: 129 us -> none  [per_device(): grad_weight = lax.psum(local_weight, ('row', 'col'))]
    all_gather x0 -> x1, waiting for transfers between devices: none -> 77.3 us  [per_device(): lax.all_gather(local_weight, axis_name=('row', 'col'))]
    reduce_sum x0 -> x1, other arithmetic: none -> 4.63 us  [per_device(): jnp.sum(lax.all_gather(local_weight, axis_name=('row', 'col')), axis=0)]
    unnamed x20 -> x19, local copies, waits for them, and re-layouts: 12.6 us -> 11 us
where the time goes in v1:
time: 376 us; the launch traced here: 375 us
  waiting for transfers between devices  162 us (43%)
  other arithmetic  82.7 us (22%)
  local copies, waits for them, and re-layouts  50.9 us (14%)
  matrix products  47.9 us (13%)
  blocking collectives  17.6 us (5%)
  between operations  13.9 us (4%)
    all_gather x1, waiting for transfers between devices, per_device(): lax.all_gather(local_weight, axis_name=('row', 'col'))  77.3 us
    dot_general x6, matrix products, one_group(): jnp.einsum(form, block_vals, picked, preferred_element_type=jnp.float32)  44.3 us
    reduce_scatter x1, waiting for transfers between devices, per_device(): lax.psum_scatter(partial_rows.reshape(row_blocks * side, width), 'col', s...  43 us
    scatter-add x1, other arithmetic, per_device(): jax.ops.segment_sum(products, row_ids, num_segments=row_blocks)  36.1 us
    scatter-add x1, other arithmetic, per_device(): jax.ops.segment_sum(back_products, col_ids, num_segments=col_blocks)  36 us
    reduce_scatter x1, waiting for transfers between devices, per_device(): lax.psum_scatter(partial_cols.reshape(col_blocks * side, width), 'row', s...  26.4 us
    another operation x2, local copies, waits for them, and re-layouts  23 us
    all_gather x1, blocking collectives, per_device(): panel = lax.all_gather(features, 'row', axis=1, tiled=True)  17.6 us
  transfers between devices with their start and end apart: 4, of which 4 were waited for; matrix products, arithmetic and copies ran while one was open for 3% of the time, Pallas kernels for 0%

profile of v1, /device:TPU:0, one launch (start us, length us, event | category | flops | bytes accessed | tf_op | source)
XLA Modules:
  0.0 374.8 jit_solution(2304256057935282639)
XLA Ops:
  7.2 17.6 %all_gather.12 = bf16[1,1024,256]{2,1,0:T(8,128)(2,1)S(1)} all-gather(bf16[1,256,256]{2,1,0:T(8,128)(2,1)} %param.11), channel_id=1, replica_groups=mesh['row'=4,'col'=8] {'row'}, dimensions={1}, use_global_device_ids=true | all-gather | bytes 655360 | tf_op jit(solution)/shard_map/all_gather | solution.py:42
  24.8 11.5 %broadcast.44.clone = f32[192,128,256]{2,1,0:T(8,128)} broadcast(f32[]{:T(128)} %constant.132.clone.1), dimensions={} | broadcast | bytes 25165828 | tf_op jit(solution)/shard_map/broadcast.3
  36.3 32.7 %while.26 = (s32[]{:T(128)}, f32[192,128,256]{2,1,0:T(8,128)}, s32[]{:T(128)}, bf16[192,128,128]{2,1,0:T(8,128)(2,1)}, s32[192]{0:T(256)S(1)}, /*index=5*/bf16[8...) while((s32[]{:T(128)}, f32[192,128,256]{2,1,0:T(8,128)}, s32[]{:T(128)}, ...), condition=%wide.region_1.0_spmd, body=%wide.region_0.1_spmd.sunk | while | flops 541066752 | bytes 23075232 | solution.py:29
  37.1 2.8 gather_fusion
  39.8 7.4 %select_dynamic-update-slice_fusion.4 = f32[192,128,256]{2,1,0:T(8,128)} fusion(f32[192,128,256]{2,1,0:T(8,128)} %get-tuple-element.358, s32[]{:T(128)S(6)} %select_n.88, pred[64]{0:T(512)(128)(4,1)S(1)} %get-tuple-element.335, bf16[64,128,256]{2,1,0:T(8,128)(2,1)} %gather_fusion, pred[64]{0:T(512)(128)(4,1)S(1)} %get-tuple-element.337, ...), kind=kOutput, calls=%fused_computation.4.clone.1 | convolution fusion | flops 541065216 | bytes 14681216 | tf_op jit(solution)/shard_map/while/body/eval_jaxpr/bij,bjf->bif/dot_general | solution.py:22
  47.9 2.8 gather_fusion
  50.7 7.4 %select_dynamic-update-slice_fusion.4 = f32[192,128,256]{2,1,0:T(8,128)} fusion(f32[192,128,256]{2,1,0:T(8,128)} %get-tuple-element.358, s32[]{:T(128)S(6)} %select_n.88, pred[64]{0:T(512)(128)(4,1)S(1)} %get-tuple-element.335, bf16[64,128,256]{2,1,0:T(8,128)(2,1)} %gather_fusion, pred[64]{0:T(512)(128)(4,1)S(1)} %get-tuple-element.337, ...), kind=kOutput, calls=%fused_computation.4.clone.1 | convolution fusion | flops 541065216 | bytes 14681216 | tf_op jit(solution)/shard_map/while/body/eval_jaxpr/bij,bjf->bif/dot_general | solution.py:22
  58.8 2.8 gather_fusion
  61.6 7.4 %select_dynamic-update-slice_fusion.4 = f32[192,128,256]{2,1,0:T(8,128)} fusion(f32[192,128,256]{2,1,0:T(8,128)} %get-tuple-element.358, s32[]{:T(128)S(6)} %select_n.88, pred[64]{0:T(512)(128)(4,1)S(1)} %get-tuple-element.335, bf16[64,128,256]{2,1,0:T(8,128)(2,1)} %gather_fusion, pred[64]{0:T(512)(128)(4,1)S(1)} %get-tuple-element.337, ...), kind=kOutput, calls=%fused_computation.4.clone.1 | convolution fusion | flops 541065216 | bytes 14681216 | tf_op jit(solution)/shard_map/while/body/eval_jaxpr/bij,bjf->bif/dot_general | solution.py:22
  69.2 36.1 %scatter_fusion = f32[16,128,256]{2,1,0:T(8,128)S(1)} fusion(f32[16,128,256]{2,1,0:T(8,128)S(1)} %broadcast_in_dim.108, s32[192]{0:T(256)S(1)} %bitcast.24, f32[192,128,256]{2,1,0:T(8,128)} %get-tuple-element.221), kind=kCustom, calls=%fused_computation.2 | custom fusion | flops 6291456 | bytes 75498240 | tf_op jit(solution)/shard_map/scatter-add | solution.py:45
  106.7 43.0 %reduce-scatter.3.cloned.1.call-done = f32[256,256]{1,0:T(8,128)} async-done(((f32[2048,256]{1,0:T(8,128)}), f32[256,256]{1,0:T(8,128)}) %reduce-scatter.3.cloned.1.call-update) | async-done | bytes 262160 | tf_op jit(solution)/shard_map/reduce_scatter | solution.py:46
  152.5 8.6 %copy.10 = bf16[1,1,192,128,128]{3,4,2,1,0:T(8,128)(2,1)} copy(bf16[1,1,192,128,128]{4,3,2,1,0:T(8,128)(2,1)} %bitcast.21) | data formatting | bytes 12582912 | tf_op args[3]
  161.0 14.9 %all-gather.4.cloned.1.call-done = bf16[2048,256]{1,0:T(8,128)(2,1)} async-done(((bf16[256,256]{1,0:T(8,128)(2,1)}), bf16[2048,256]{1,0:T(8,128)(2,1)}) %all-gather.4.cloned.1.call-update) | async-done | bytes 1048592 | tf_op jit(solution)/shard_map/all_gather | solution.py:63
  176.0 11.5 %broadcast.44 = f32[192,128,256]{2,1,0:T(8,128)} broadcast(f32[]{:T(128)} %constant.132.clone.1), dimensions={} | broadcast | bytes 25165828 | tf_op jit(solution)/shard_map/broadcast.3
  187.4 32.7 %while.27 = (s32[]{:T(128)}, f32[192,128,256]{2,1,0:T(8,128)}, s32[]{:T(128)}, bf16[192,128,128]{1,2,0:T(8,128)(2,1)}, s32[192]{0:T(256)S(1)}, /*index=5*/bf16[1...) while((s32[]{:T(128)}, f32[192,128,256]{2,1,0:T(8,128)}, s32[]{:T(128)}, ...), condition=%wide.region_6.7_spmd, body=%wide.region_5.6_spmd.sunk | while | flops 541066752 | bytes 23075232 | solution.py:29
  188.2 2.8 gather_fusion.1
  191.0 7.4 %select_dynamic-update-slice_fusion.5 = f32[192,128,256]{2,1,0:T(8,128)} fusion(f32[192,128,256]{2,1,0:T(8,128)} %get-tuple-element.388, s32[]{:T(128)S(6)} %select_n.91, pred[64]{0:T(512)(128)(4,1)S(1)} %get-tuple-element.344, bf16[64,128,256]{2,1,0:T(8,128)(2,1)} %gather_fusion.1, pred[64]{0:T(512)(128)(4,1)S(1)} %get-tuple-element.346, ...), kind=kOutput, calls=%fused_computation.16.clone.1 | convolution fusion | flops 541065216 | bytes 14681216 | tf_op jit(solution)/shard_map/while/body/eval_jaxpr/bji,bjf->bif/dot_general | solution.py:22
  199.1 2.8 gather_fusion.1
  201.8 7.4 %select_dynamic-update-slice_fusion.5 = f32[192,128,256]{2,1,0:T(8,128)} fusion(f32[192,128,256]{2,1,0:T(8,128)} %get-tuple-element.388, s32[]{:T(128)S(6)} %select_n.91, pred[64]{0:T(512)(128)(4,1)S(1)} %get-tuple-element.344, bf16[64,128,256]{2,1,0:T(8,128)(2,1)} %gather_fusion.1, pred[64]{0:T(512)(128)(4,1)S(1)} %get-tuple-element.346, ...), kind=kOutput, calls=%fused_computation.16.clone.1 | convolution fusion | flops 541065216 | bytes 14681216 | tf_op jit(solution)/shard_map/while/body/eval_jaxpr/bji,bjf->bif/dot_general | solution.py:22
  212.7 7.4 %select_dynamic-update-slice_fusion.5 = f32[192,128,256]{2,1,0:T(8,128)} fusion(f32[192,128,256]{2,1,0:T(8,128)} %get-tuple-element.388, s32[]{:T(128)S(6)} %select_n.91, pred[64]{0:T(512)(128)(4,1)S(1)} %get-tuple-element.344, bf16[64,128,256]{2,1,0:T(8,128)(2,1)} %gather_fusion.1, pred[64]{0:T(512)(128)(4,1)S(1)} %get-tuple-element.346, ...), kind=kOutput, calls=%fused_computation.16.clone.1 | convolution fusion | flops 541065216 | bytes 14681216 | tf_op jit(solution)/shard_map/while/body/eval_jaxpr/bji,bjf->bif/dot_general | solution.py:22
  220.2 36.0 %scatter_fusion.1 = f32[8,128,256]{2,1,0:T(8,128)S(1)} fusion(f32[8,128,256]{2,1,0:T(8,128)S(1)} %broadcast_in_dim.109, s32[192]{0:T(256)S(1)} %get-tuple-element.424, f32[192,128,256]{2,1,0:T(8,128)} %get-tuple-element.222), kind=kCustom, calls=%fused_computation.3 | custom fusion | flops 6291456 | bytes 75498240 | tf_op jit(solution)/shard_map/scatter-add | solution.py:66
  258.3 26.4 %reduce-scatter.5.cloned.1.call-done = f32[256,256]{1,0:T(8,128)} async-done(((f32[1024,256]{1,0:T(8,128)}), f32[256,256]{1,0:T(8,128)}) %reduce-scatter.5.cloned.1.call-update) | async-done | bytes 262160 | tf_op jit(solution)/shard_map/reduce_scatter | solution.py:67
  286.4 77.3 %all-gather.6.cloned.1.call-done = f32[8192,256]{1,0:T(8,128)} async-done(((f32[256,256]{1,0:T(8,128)}), f32[8192,256]{1,0:T(8,128)}) %all-gather.6.cloned.1.call-update) | async-done | bytes 8388624 | tf_op jit(solution)/shard_map/all_gather | solution.py:59
  363.6 4.6 %reduce_sum.9 = f32[256,256]{1,0:T(8,128)} reduce(f32[32,256,256]{2,1,0:T(8,128)} %bitcast.23, f32[]{:T(128)} %constant.132.clone.1), dimensions={0}, to_apply=%region_4.5 | reduce | flops 2031616 | bytes 8650756 | tf_op jit(solution)/shard_map/reduce_sum | solution.py:59
  (45 shorter events, 15.4 us)
Async XLA Ops:
  7.2 142.5 %copy-start = (bf16[256,256]{1,0:T(8,128)(2,1)S(1)}, bf16[256,256]{1,0:T(8,128)(2,1)}, u32[]{:S(2)}) copy-start(bf16[256,256]{1,0:T(8,128)(2,1)} %param.12) | copy-start | bytes 393220
  7.2 142.5 %reduce-scatter.3.cloned.1.call-start = ((), (), s32[]{:S(2)}) async-start(), calls=%async_computation.2 | async-start | bytes 2359296 | tf_op jit(solution)/shard_map/reduce_scatter | solution.py:46
  24.8 11.5 %copy-start.7 = (s32[1,1,192]{2,1,0:T(1,128)S(1)}, s32[1,1,192]{2,1,0:T(1,128)}, u32[]{:S(2)}) copy-start(s32[1,1,192]{2,1,0:T(1,128)} %param.16) | copy-start | bytes 2308
  36.3 32.9 %copy-start.6 = (s32[1,1,192]{2,1,0:T(1,128)S(1)}, s32[1,1,192]{2,1,0:T(1,128)}, u32[]{:S(2)}) copy-start(s32[1,1,192]{2,1,0:T(1,128)} %param.15) | copy-start | bytes 2308
  69.2 80.4 %copy-start.8 = (bf16[256,256]{1,0:T(8,128)(2,1)S(1)}, bf16[256,256]{1,0:T(8,128)(2,1)}, u32[]{:S(2)}) copy-start(bf16[256,256]{1,0:T(8,128)(2,1)} %param.13) | copy-start | bytes 393220
  105.3 1.3 copy-start.4
  106.6 69.3 %all-gather.4.cloned.1.call-start = ((), (), s32[]{:S(2)}) async-start(), calls=%async_computation.3 | async-start | bytes 1179648 | tf_op jit(solution)/shard_map/all_gather | solution.py:63
  152.4 132.3 %reduce-scatter.5.cloned.1.call-start = ((), (), s32[]{:S(2)}) async-start(), calls=%async_computation.4 | async-start | bytes 1310720 | tf_op jit(solution)/shard_map/reduce_scatter | solution.py:67
  176.0 11.5 %copy-start.3 = (bf16[2048,256]{1,0:T(8,128)(2,1)S(1)}, bf16[2048,256]{1,0:T(8,128)(2,1)}, u32[]{:S(2)}) copy-start(bf16[2048,256]{1,0:T(8,128)(2,1)} %all-gather.4.cloned.1.call-done) | copy-start | bytes 3145732
  220.2 37.2 %copy-start.5 = (f32[256,256]{1,0:T(8,128)S(1)}, f32[256,256]{1,0:T(8,128)}, u32[]{:S(2)}) copy-start(f32[256,256]{1,0:T(8,128)} %reduce-scatter.3.cloned.1.call-done) | copy-start | bytes 786436
  220.2 148.1 %copy-start.1 = (bf16[256,256]{1,0:T(8,128)(2,1)S(1)}, bf16[256,256]{1,0:T(8,128)(2,1)}, u32[]{:S(2)}) copy-start(bf16[256,256]{1,0:T(8,128)(2,1)} %param.12) | copy-start | bytes 393220
  256.2 1.1 copy-start.2
  257.3 106.3 %all-gather.6.cloned.1.call-start = ((), (), s32[]{:S(2)}) async-start(), calls=%async_computation.5 | async-start | bytes 8650752 | tf_op jit(solution)/shard_map/all_gather | solution.py:59
Sparse Core Ops, SparseCore 0:
  106.7 42.8 reduce-scatter.2
  152.6 23.3 all-gather.3
  257.4 27.2 reduce-scatter.4
  288.0 75.5 all-gather.5
